TPU v7x, 32 devices: a whole 2x2x4 slice. The times are simulated.
32 devices in a mesh: rows: 16 (over z, y, core), cols: 2 (over x).
Axes of the slice: x: 2, y: 2, z: 4, core: 2. Of those that a mesh axis runs over, the one named last changes fastest.
Arguments:
- features: bfloat16 [4096, 128], P('rows', 'cols'), may hold values from -6 to 6
- adj_tiles: bfloat16 [1536, 128, 128], P('rows'), may hold values from -0.109375 to 0.109375
- tile_src: int32 [1536], P('rows'), may hold values from 0 to 31, as said below
- tile_dst: int32 [1536], P('rows'), may hold values from 0 to 1, as said below
- tile_count: int32 [16], P('rows'), may hold values from 24 to 96, as said below
- cluster_size: int32 [32], P('rows'), may hold values from 64 to 128, as said below
- weight: bfloat16 [128, 256], P(None, 'cols'), may hold values from -0.5 to 0.5
- bias: float32 [256], P('cols'), may hold values from -3 to 3
- grad_out: bfloat16 [4096, 256], P('rows', 'cols'), may hold values from -6 to 6
Outputs:
- hidden: bfloat16 [4096, 256], P('rows', 'cols')
- grad_weight: float32 [128, 256], P(None, 'cols')
- grad_bias: float32 [256], P('cols')
- grad_features: bfloat16 [4096, 128], P('rows', 'cols')
Inputs may be any that keep to these rules, and one draw needn't show every extreme that they name: In row group r, slots 0 to tile_count[r] - 1 of its 96 slots hold tiles, in non-decreasing order of tile_src; the later slots are unused: their tile_src and tile_dst hold 0, and their adj_tiles hold arbitrary values that must not contribute. A used slot's column cluster belongs to row group r itself or to a row group whose index differs from r in exactly one bit (row group g holds clusters g * 2 to g * 2 + 1). Equal (row, column) pairs may repeat and then add. `tile_dst`: unused slots hold 0. `tile_count`: some row groups use all 96 slots. `cluster_size`: the real nodes of a cluster are its first ones; some cluster is full.
All inputs are finite; a program needn't handle non-finite values.
Results may differ from a plain program's by a relative error of at most 0.006.
Values may be sent and summed in bfloat16 or wider, within the bound.
No kernel may reach another device: no remote copies, remote signals or barrier semaphores. Data moves between devices by JAX's collectives and lax.ppermute only.
A program may use at most 64 MiB of HBM per device.

v0:
```python
import math
import jax
import jax.numpy as jnp
from jax import lax
from jax.sharding import PartitionSpec as P

TILE_GROUP = 16


def partner(shard, axis, distance):
    return lax.ppermute(shard, axis, [(i, i ^ 1 << distance) for i in range(lax.axis_size(axis))])


def sweep_slots(first_slot, last_slot, work, totals):
    turn_count = (last_slot - first_slot + TILE_GROUP - 1) // TILE_GROUP

    def one_turn(turn_index, carried):
        slot_ids = first_slot + turn_index * TILE_GROUP + jnp.arange(TILE_GROUP, dtype=jnp.int32)
        return work(carried, slot_ids, slot_ids < last_slot)

    return lax.fori_loop(0, jnp.maximum(turn_count, 0), one_turn, totals)


def slot_bounds(sources, first_slot, last_slot, low_cluster, high_cluster):
    positions = jnp.arange(sources.shape[0], dtype=jnp.int32)
    inside = (positions >= first_slot) & (positions < last_slot)
    below_low = jnp.sum((inside & (sources < low_cluster)).astype(jnp.int32))
    below_high = jnp.sum((inside & (sources < high_cluster)).astype(jnp.int32))
    return (first_slot + below_low, first_slot + below_high)


def neighbour_slots(sources, own_group, per_group, levels):
    group_of = sources // per_group
    within = sources - group_of * per_group
    differs = jnp.bitwise_xor(group_of, own_group)
    level = jnp.zeros_like(sources)
    for bit in range(levels):
        level = level + (bit + 1) * (differs == 1 << bit).astype(jnp.int32)
    return level * per_group + within


def gather_products(
    totals, tile_data, sources, targets, slot_ids, is_valid, row_table, base_cluster
):
    clamped = jnp.minimum(slot_ids, tile_data.shape[0] - 1)
    tile_block = tile_data[clamped]
    from_rows = jnp.clip(sources[clamped] - base_cluster, 0, row_table.shape[0] - 1)
    products = jnp.einsum(
        "tij,tjf->tif", tile_block, row_table[from_rows], preferred_element_type=jnp.float32
    )
    placed = jnp.where(is_valid, targets[clamped], totals.shape[0])
    return totals.at[placed].add(products, mode="drop")


def spread_products(
    totals, tile_data, sources, targets, slot_ids, is_valid, grad_table, base_cluster
):
    clamped = jnp.minimum(slot_ids, tile_data.shape[0] - 1)
    tile_block = tile_data[clamped]
    products = jnp.einsum(
        "tji,tjf->tif", tile_block, grad_table[targets[clamped]], preferred_element_type=jnp.float32
    )
    placed = jnp.where(is_valid, sources[clamped] - base_cluster, totals.shape[0])
    return totals.at[placed].add(products, mode="drop")


def local(
    features, adj_tiles, tile_src, tile_dst, tile_count, cluster_size, weight, bias, grad_out
):
    clusters_here = cluster_size.shape[0]
    tile_width = adj_tiles.shape[1]
    feat_half = features.shape[1]
    node_rows = clusters_here * tile_width
    node_ids = jnp.arange(tile_width, dtype=jnp.int32)
    live_node = (node_ids[None, :] < cluster_size[:, None]).astype(jnp.float32)[:, :, None]
    live_flat = live_node.reshape(node_rows, 1)
    masked = (
        features.reshape(clusters_here, tile_width, feat_half).astype(jnp.float32) * live_node
    ).astype(jnp.bfloat16)
    my_count = tile_count[0]
    levels = lax.axis_size("rows").bit_length() - 1
    local_slots = neighbour_slots(tile_src, lax.axis_index("rows"), clusters_here, levels)
    zero_totals = jnp.zeros((clusters_here, tile_width, feat_half), jnp.float32)
    whole_rows = lax.all_gather(masked, "rows", axis=0, tiled=True)
    row_count = whole_rows.shape[0]
    first_slot, last_slot = slot_bounds(tile_src, 0, my_count, 0, 0 + row_count)
    own_totals = sweep_slots(
        first_slot,
        last_slot,
        lambda totals, slot_ids, is_valid: gather_products(
            totals, adj_tiles, tile_src, tile_dst, slot_ids, is_valid, whole_rows, 0
        ),
        zero_totals,
    )
    agg_local = own_totals.reshape(node_rows, feat_half).astype(jnp.bfloat16)
    agg_full = lax.all_gather(agg_local, "cols", axis=1, tiled=True)
    pre_activation = jnp.dot(agg_full, weight, preferred_element_type=jnp.float32) + bias
    sigmoid_pre = jax.nn.sigmoid(pre_activation)
    hidden = (pre_activation * sigmoid_pre * live_flat).astype(jnp.bfloat16)
    grad_pre = (
        grad_out.astype(jnp.float32)
        * sigmoid_pre
        * (1.0 + pre_activation * (1.0 - sigmoid_pre))
        * live_flat
    ).astype(jnp.bfloat16)
    weight_term = lax.dot_general(
        agg_full, grad_pre, (((0,), (0,)), ((), ())), preferred_element_type=jnp.float32
    )
    bias_term = jnp.sum(grad_pre.astype(jnp.float32), axis=0)
    weight_total, bias_total = lax.psum((weight_term, bias_term), "rows")
    grad_scale = 1.0 / math.sqrt(node_rows * lax.axis_size("rows"))
    grad_weight = weight_total * grad_scale
    grad_bias = bias_total * grad_scale
    partial_value = lax.dot_general(
        grad_pre, weight, (((1,), (1,)), ((), ())), preferred_element_type=jnp.float32
    )
    grad_agg = (
        lax.psum_scatter(partial_value, "cols", scatter_dimension=1, tiled=True)
        .astype(jnp.bfloat16)
        .reshape(clusters_here, tile_width, feat_half)
    )
    buckets = jnp.zeros(((levels + 1) * clusters_here, tile_width, feat_half), jnp.float32)
    buckets = sweep_slots(
        0,
        my_count,
        lambda carried, slot_ids, is_valid: spread_products(
            carried, adj_tiles, local_slots, tile_dst, slot_ids, is_valid, grad_agg, 0
        ),
        buckets,
    )
    summed = buckets[:clusters_here]
    for bit in range(levels):
        summed = summed + partner(
            buckets[(bit + 1) * clusters_here : (bit + 2) * clusters_here], "rows", bit
        )
    grad_features = (summed * live_node).reshape(node_rows, feat_half).astype(jnp.bfloat16)
    return (hidden, grad_weight, grad_bias, grad_features)


def solution(mesh):
    return jax.shard_map(
        local,
        mesh=mesh,
        in_specs=(
            P("rows", "cols"),
            P("rows", None, None),
            P("rows"),
            P("rows"),
            P("rows"),
            P("rows"),
            P(None, "cols"),
            P("cols"),
            P("rows", "cols"),
        ),
        out_specs=(P("rows", "cols"), P(None, "cols"), P("cols"), P("rows", "cols")),
        check_vma=False,
    )
```

profile of v0, /device:TPU:8, one launch (start us, length us, event | category | flops | bytes accessed | tf_op | source)
XLA Modules:
  0.0 193.4 jit_solution(5257428830742332566)
XLA Ops:
  12.9 20.3 %all_gather.6 = bf16[32,128,64]{1,2,0:T(8,128)(2,1)S(1)} all-gather(bf16[2,128,64]{1,2,0:T(8,128)(2,1)S(1)} %copy.30), channel_id=1, replica_groups=mesh['rows'=16,'cols'=2] {'rows'}, dimensions={0}, use_global_device_ids=true | all-gather | bytes 557056 | tf_op jit(solution)/shard_map/all_gather | solution.py:84
  33.8 27.2 %while.20 = (s32[]{:T(128)}, f32[2,128,64]{1,2,0:T(8,128)S(1)}, s32[]{:T(128)}, s32[]{:T(128)}, s32[]{:T(128)}, /*index=5*/s32[96]{0:T(128)}, bf16[96,128,128]{2...) while((s32[]{:T(128)}, f32[2,128,64]{1,2,0:T(8,128)S(1)}, ...), condition=%wide.region_4.5_spmd, body=%wide.region_2.4_spmd.sunk | while | flops 33687796 | bytes 4465817 | solution.py:21
  34.5 1.3 gather_fusion
  36.4 2.5 %gather_fusion.1 = bf16[16,128,128]{2,1,0:T(8,128)(2,1)S(1)} fusion(bf16[96,128,128]{2,1,0:T(8,128)(2,1)} %get-tuple-element.328, s32[1024]{0:T(1024)S(1)} %pad_clamp_fusion.8), kind=kCustom, calls=%fused_computation.1.clone.1 | custom fusion | bytes 1048640 | tf_op jit(solution)/shard_map/while/body/gather | solution.py:46
  39.0 1.3 gather_fusion.2
  41.5 1.4 scatter_fusion
  45.5 2.5 %gather_fusion.1 = bf16[16,128,128]{2,1,0:T(8,128)(2,1)S(1)} fusion(bf16[96,128,128]{2,1,0:T(8,128)(2,1)} %get-tuple-element.328, s32[1024]{0:T(1024)S(1)} %pad_clamp_fusion.8), kind=kCustom, calls=%fused_computation.1.clone.1 | custom fusion | bytes 1048640 | tf_op jit(solution)/shard_map/while/body/gather | solution.py:46
  50.5 1.4 scatter_fusion
  54.6 2.5 %gather_fusion.1 = bf16[16,128,128]{2,1,0:T(8,128)(2,1)S(1)} fusion(bf16[96,128,128]{2,1,0:T(8,128)(2,1)} %get-tuple-element.328, s32[1024]{0:T(1024)S(1)} %pad_clamp_fusion.8), kind=kCustom, calls=%fused_computation.1.clone.1 | custom fusion | bytes 1048640 | tf_op jit(solution)/shard_map/while/body/gather | solution.py:46
  59.6 1.4 scatter_fusion
  61.0 4.6 %all_gather.7 = bf16[256,128]{0,1:T(8,128)(2,1)S(1)} all-gather(bf16[256,64]{0,1:T(8,128)(2,1)S(1)} %copy_bitcast_fusion.1), channel_id=1, replica_groups=mesh['rows'=16,'cols'=2] {'cols'}, dimensions={1}, use_global_device_ids=true | all-gather | bytes 98304 | tf_op jit(solution)/shard_map/all_gather | solution.py:96
  68.2 48.7 %psum.15 = f32[128]{0:T(128)S(1)} all-reduce(f32[128]{0:T(128)S(1)} %get-tuple-element.184), channel_id=1, replica_groups=mesh['rows'=16,'cols'=2] {'rows'}, use_global_device_ids=true, to_apply=%region_7.8 | all-reduce | flops 128 | bytes 1024 | tf_op jit(solution)/shard_map/psum | solution.py:110
  118.4 22.8 %while.21 = (s32[]{:T(128)}, f32[10,128,64]{1,2,0:T(8,128)S(1)}, s32[]{:T(128)}, s32[]{:T(128)}, s32[96]{0:T(128)S(1)}, /*index=5*/bf16[96,128,128]{2,1,0:T(8,12...) while((s32[]{:T(128)}, f32[10,128,64]{1,2,0:T(8,128)S(1)}, s32[]{:T(128)}, ...), condition=%wide.region_11.12_spmd, body=%wide.region_9.11_spmd.sunk | while | flops 33687776 | bytes 4465797 | solution.py:21
  119.8 2.5 %gather_fusion.5 = bf16[16,128,128]{2,1,0:T(8,128)(2,1)S(1)} fusion(bf16[96,128,128]{2,1,0:T(8,128)(2,1)} %get-tuple-element.358, s32[1024]{0:T(1024)S(1)} %pad_clamp_fusion.10), kind=kCustom, calls=%fused_computation.5.clone.1 | custom fusion | bytes 1048640 | tf_op jit(solution)/shard_map/while/body/gather | solution.py:59
  122.3 1.3 gather_fusion.6
  124.6 1.3 scatter_fusion.1
  127.4 2.5 %gather_fusion.5 = bf16[16,128,128]{2,1,0:T(8,128)(2,1)S(1)} fusion(bf16[96,128,128]{2,1,0:T(8,128)(2,1)} %get-tuple-element.358, s32[1024]{0:T(1024)S(1)} %pad_clamp_fusion.10), kind=kCustom, calls=%fused_computation.5.clone.1 | custom fusion | bytes 1048640 | tf_op jit(solution)/shard_map/while/body/gather | solution.py:59
  132.2 1.4 scatter_fusion.1
  134.9 2.6 %gather_fusion.5 = bf16[16,128,128]{2,1,0:T(8,128)(2,1)S(1)} fusion(bf16[96,128,128]{2,1,0:T(8,128)(2,1)} %get-tuple-element.358, s32[1024]{0:T(1024)S(1)} %pad_clamp_fusion.10), kind=kCustom, calls=%fused_computation.5.clone.1 | custom fusion | bytes 1048640 | tf_op jit(solution)/shard_map/while/body/gather | solution.py:59
  137.5 1.3 gather_fusion.6
  139.8 1.3 scatter_fusion.1
  141.6 23.7 %collective-permute-start.2 = (f32[2,128,64]{1,0,2:T(2,128)S(1)}, f32[2,128,64]{1,0,2:T(2,128)S(1)}, u32[]{:S(2)}, u32[]{:S(2)}) collective-permute-start(f32[2,128,64]{1,0,2:T(2,128)S(1)} %get-tuple-element.188), channel_id=1, source_target_pairs={{0,8},{2,10},{4,12},{6,14},{8,0},{10,2},{12,4},{14,6},{16,24},{18,... | collective-permute-start | bytes 196616 | tf_op jit(solution)/shard_map/ppermute | solution.py:11
  165.2 18.5 %all-reduce.2.cloned.1.call-done = f32[128,128]{1,0:T(8,128)} async-done(((f32[128,128]{1,0:T(8,128)}), f32[128,128]{1,0:T(8,128)}) %all-reduce.2.cloned.1.call-update) | async-done | bytes 65552 | tf_op jit(solution)/shard_map/psum | solution.py:110
  183.7 1.5 broadcast_multiply_fusion
  (87 shorter events, 27.5 us)
Async XLA Ops:
  8.0 57.6 %copy-start = (bf16[128,128]{1,0:T(8,128)(2,1)S(1)}, bf16[128,128]{1,0:T(8,128)(2,1)}, u32[]{:S(2)}) copy-start(bf16[128,128]{1,0:T(8,128)(2,1)} %param.19) | copy-start | bytes 98308
  8.0 109.4 %reduce-scatter.2.cloned.1.call-start = ((), (), s32[]{:S(2)}) async-start(), calls=%async_computation.2 | async-start | bytes 196608 | tf_op jit(solution)/shard_map/reduce_scatter | solution.py:118
  33.7 31.8 %copy-start.1 = (bf16[256,128]{1,0:T(8,128)(2,1)S(1)}, bf16[256,128]{1,0:T(8,128)(2,1)}, u32[]{:S(2)}) copy-start(bf16[256,128]{1,0:T(8,128)(2,1)} %param.21) | copy-start | bytes 196612
  33.7 31.8 %copy-start.2 = (f32[128]{0:T(128)S(1)}, f32[128]{0:T(128)}, u32[]{:S(2)}) copy-start(f32[128]{0:T(128)} %param.20) | copy-start | bytes 1540
  67.3 116.4 %all-reduce.2.cloned.1.call-start = ((), (), s32[]{:S(2)}) async-start(), calls=%async_computation.1 | async-start | bytes 131072 | tf_op jit(solution)/shard_map/psum | solution.py:110
  141.5 43.7 %collective-permute-start.3 = (f32[2,128,64]{1,0,2:T(2,128)S(1)}, f32[2,128,64]{1,0,2:T(2,128)S(1)}, u32[]{:S(2)}, u32[]{:S(2)}) collective-permute-start(f32[2,128,64]{1,0,2:T(2,128)S(1)} %get-tuple-element.187), channel_id=1, source_target_pairs={{0,16},{2,18},{4,20},{6,22},{8,24},{10,26},{12,28},{14,30},{16,0},... | collective-permute-start | bytes 196616 | tf_op jit(solution)/shard_map/ppermute | solution.py:11
  141.6 43.6 %collective-permute-start.2 = (f32[2,128,64]{1,0,2:T(2,128)S(1)}, f32[2,128,64]{1,0,2:T(2,128)S(1)}, u32[]{:S(2)}, u32[]{:S(2)}) collective-permute-start(f32[2,128,64]{1,0,2:T(2,128)S(1)} %get-tuple-element.188), channel_id=1, source_target_pairs={{0,8},{2,10},{4,12},{6,14},{8,0},{10,2},{12,4},{14,6},{16,24},{18,... | collective-permute-start | bytes 196616 | tf_op jit(solution)/shard_map/ppermute | solution.py:11
  165.2 20.0 %collective-permute-start.1 = (f32[2,128,64]{1,0,2:T(2,128)S(1)}, f32[2,128,64]{1,0,2:T(2,128)S(1)}, u32[]{:S(2)}, u32[]{:S(2)}) collective-permute-start(f32[2,128,64]{1,0,2:T(2,128)S(1)} %get-tuple-element.189), channel_id=1, source_target_pairs={{0,4},{2,6},{4,0},{6,2},{8,12},{10,14},{12,8},{14,10},{16,20},{18,... | collective-permute-start | bytes 196616 | tf_op jit(solution)/shard_map/ppermute | solution.py:11
  165.2 20.0 %collective-permute-start = (f32[2,128,64]{1,0,2:T(2,128)S(1)}, f32[2,128,64]{1,0,2:T(2,128)S(1)}, u32[]{:S(2)}, u32[]{:S(2)}) collective-permute-start(f32[2,128,64]{1,0,2:T(2,128)S(1)} %get-tuple-element.186), channel_id=1, source_target_pairs={{0,2},{2,0},{4,6},{6,4},{8,10},{10,8},{12,14},{14,12},{16,18},{18,... | collective-permute-start | bytes 196616 | tf_op jit(solution)/shard_map/ppermute | solution.py:11
Sparse Core Ops, SparseCore 0:
  67.4 33.8 reduce-scatter.1
Sparse Core Ops, SparseCore 1:
  71.8 111.9 all-reduce.1
where the time goes:
time: 195 us; the launch traced here: 193 us
  blocking collectives  73.6 us (38%)
  local copies, waits for them, and re-layouts  35.4 us (18%)
  starting transfers between devices  23.8 us (12%)
  waiting for transfers between devices  18.5 us (9%)
  between operations  17.6 us (9%)
  other arithmetic  17.2 us (9%)
  matrix products  4.85 us (2%)
  loops' own time  2.36 us (1%)
    psum x1, blocking collectives, local(): weight_total, bias_total = lax.psum((weight_term, bias_term), 'rows')  48.7 us
    ppermute x4, starting transfers between devices, partner(): lax.ppermute(shard, axis, [(i, i ^ 1 << distance) for i in range(lax.axis...  23.7 us
    all_gather x1, blocking collectives, local(): whole_rows = lax.all_gather(masked, 'rows', axis=0, tiled=True)  20.3 us
    psum x1, waiting for transfers between devices, local(): weight_total, bias_total = lax.psum((weight_term, bias_term), 'rows')  18.5 us
    gather x3, local copies, waits for them, and re-layouts, spread_products(): tile_block = tile_data[clamped]  7.64 us
    gather x3, local copies, waits for them, and re-layouts, gather_products(): tile_block = tile_data[clamped]  7.62 us
    all_gather x1, blocking collectives, local(): agg_full = lax.all_gather(agg_local, 'cols', axis=1, tiled=True)  4.58 us
    scatter-add x3, other arithmetic, gather_products(): return totals.at[placed].add(products, mode='drop')  4.07 us
  transfers between devices with their start and end apart: 6, of which 1 were waited for; matrix products, arithmetic and copies ran while one was open for 14% of the time, Pallas kernels for 0%

commit v1 on v0

--- a/solution.py
+++ b/solution.py
@@ -81,7 +81,12 @@
     levels = lax.axis_size("rows").bit_length() - 1
     local_slots = neighbour_slots(tile_src, lax.axis_index("rows"), clusters_here, levels)
     zero_totals = jnp.zeros((clusters_here, tile_width, feat_half), jnp.float32)
-    whole_rows = lax.all_gather(masked, "rows", axis=0, tiled=True)
+    ring = [masked]
+    for hop in range(15):
+        ring.append(lax.ppermute(ring[-1], "rows", [(dev, (dev + 1) % 16) for dev in range(16)]))
+    whole_rows = jnp.roll(
+        jnp.concatenate(ring[::-1], axis=0), (lax.axis_index("rows") + 1) * ring[0].shape[0], axis=0
+    )
     row_count = whole_rows.shape[0]
     first_slot, last_slot = slot_bounds(tile_src, 0, my_count, 0, 0 + row_count)
     own_totals = sweep_slots(

time: 195 us -> 268 us (1.37)
  waiting for transfers between devices: 18.5 us -> 115 us
  blocking collectives: 73.6 us -> 53.5 us
  local copies, waits for them, and re-layouts: 35.4 us -> 31.8 us
    ppermute x0 -> x15, waiting for transfers between devices: none -> 69.3 us  [local(): lax.ppermute(ring[-1], 'rows', [(dev, (dev + 1) % 16) for dev in range(16)])]
    all_gather x1 -> x0, blocking collectives: 20.3 us -> none  [local(): whole_rows = lax.all_gather(masked, 'rows', axis=0, tiled=True)]
    psum x1, waiting for transfers between devices: 18.5 us -> 36.4 us  [local(): weight_total, bias_total = lax.psum((weight_term, bias_term), 'rows')]
    reduce_scatter x1, waiting for transfers between devices: 0.01 us -> 9.32 us  [local(): lax.psum_scatter(partial_value, 'cols', scatter_dimension=1, tiled=True)]
  transfers between devices with their start and end apart: 6 -> 21, of which waited for: 1 -> 17; matrix products, arithmetic and copies ran while one was open for 14% -> 10% of each run, Pallas kernels for 0% -> 0%
where the time goes in v1:
time: 268 us; the launch traced here: 267 us
  waiting for transfers between devices  115 us (43%)
  blocking collectives  53.5 us (20%)
  local copies, waits for them, and re-layouts  31.8 us (12%)
  starting transfers between devices  24 us (9%)
  between operations  17.7 us (7%)
  other arithmetic  17.2 us (6%)
  matrix products  4.85 us (2%)
    ppermute x15, waiting for transfers between devices, local(): lax.ppermute(ring[-1], 'rows', [(dev, (dev + 1) % 16) for dev in range(16)])  69.3 us
    psum x1, blocking collectives, local(): weight_total, bias_total = lax.psum((weight_term, bias_term), 'rows')  48.9 us
    psum x1, waiting for transfers between devices, local(): weight_total, bias_total = lax.psum((weight_term, bias_term), 'rows')  36.4 us
    ppermute x4, starting transfers between devices, partner(): lax.ppermute(shard, axis, [(i, i ^ 1 << distance) for i in range(lax.axis...  23.8 us
    reduce_scatter x1, waiting for transfers between devices, local(): lax.psum_scatter(partial_value, 'cols', scatter_dimension=1, tiled=True)  9.32 us
    gather x3, local copies, waits for them, and re-layouts, spread_products(): tile_block = tile_data[clamped]  7.66 us
    gather x3, local copies, waits for them, and re-layouts, gather_products(): tile_block = tile_data[clamped]  7.62 us
  transfers between devices with their start and end apart: 21, of which 17 were waited for; matrix products, arithmetic and copies ran while one was open for 10% of the time, Pallas kernels for 0%

profile of v1, /device:TPU:8, one launch (start us, length us, event | category | flops | bytes accessed | tf_op | source)
XLA Modules:
  0.0 266.5 jit_solution(16894380970347908411)
XLA Ops:
  9.7 4.2 %collective-permute-done = bf16[2,128,64]{1,0,2:T(2,128)(2,1)S(1)} collective-permute-done((bf16[2,128,64]{1,0,2:T(2,128)(2,1)S(1)}, bf16[2,128,64]{1,0,2:T(2,128)(2,1)S(1)}, u32[]{:S(2)}, u32[]{:S(2)}) %collective-permute-start) | collective-permute-done | bytes 32800 | tf_op jit(solution)/shard_map/ppermute | solution.py:86
  13.9 4.2 %collective-permute-done.1 = bf16[2,128,64]{1,0,2:T(2,128)(2,1)S(1)} collective-permute-done((bf16[2,128,64]{1,0,2:T(2,128)(2,1)S(1)}, bf16[2,128,64]{1,0,2:T(2,128)(2,1)S(1)}, u32[]{:S(2)}, u32[]{:S(2)}) %collective-permute-start.1) | collective-permute-done | bytes 32800 | tf_op jit(solution)/shard_map/ppermute | solution.py:86
  18.2 4.2 %collective-permute-done.2 = bf16[2,128,64]{1,0,2:T(2,128)(2,1)S(1)} collective-permute-done((bf16[2,128,64]{1,0,2:T(2,128)(2,1)S(1)}, bf16[2,128,64]{1,0,2:T(2,128)(2,1)S(1)}, u32[]{:S(2)}, u32[]{:S(2)}) %collective-permute-start.2) | collective-permute-done | bytes 32800 | tf_op jit(solution)/shard_map/ppermute | solution.py:86
  22.4 4.2 %collective-permute-done.3 = bf16[2,128,64]{1,0,2:T(2,128)(2,1)S(1)} collective-permute-done((bf16[2,128,64]{1,0,2:T(2,128)(2,1)S(1)}, bf16[2,128,64]{1,0,2:T(2,128)(2,1)S(1)}, u32[]{:S(2)}, u32[]{:S(2)}) %collective-permute-start.3) | collective-permute-done | bytes 32800 | tf_op jit(solution)/shard_map/ppermute | solution.py:86
  26.6 4.2 %collective-permute-done.4 = bf16[2,128,64]{1,0,2:T(2,128)(2,1)S(1)} collective-permute-done((bf16[2,128,64]{1,0,2:T(2,128)(2,1)S(1)}, bf16[2,128,64]{1,0,2:T(2,128)(2,1)S(1)}, u32[]{:S(2)}, u32[]{:S(2)}) %collective-permute-start.4) | collective-permute-done | bytes 32800 | tf_op jit(solution)/shard_map/ppermute | solution.py:86
  30.9 4.2 %collective-permute-done.5 = bf16[2,128,64]{1,0,2:T(2,128)(2,1)S(1)} collective-permute-done((bf16[2,128,64]{1,0,2:T(2,128)(2,1)S(1)}, bf16[2,128,64]{1,0,2:T(2,128)(2,1)S(1)}, u32[]{:S(2)}, u32[]{:S(2)}) %collective-permute-start.5) | collective-permute-done | bytes 32800 | tf_op jit(solution)/shard_map/ppermute | solution.py:86
  35.1 4.2 %collective-permute-done.6 = bf16[2,128,64]{1,0,2:T(2,128)(2,1)S(1)} collective-permute-done((bf16[2,128,64]{1,0,2:T(2,128)(2,1)S(1)}, bf16[2,128,64]{1,0,2:T(2,128)(2,1)S(1)}, u32[]{:S(2)}, u32[]{:S(2)}) %collective-permute-start.6) | collective-permute-done | bytes 32800 | tf_op jit(solution)/shard_map/ppermute | solution.py:86
  39.4 4.2 %collective-permute-done.7 = bf16[2,128,64]{1,0,2:T(2,128)(2,1)S(1)} collective-permute-done((bf16[2,128,64]{1,0,2:T(2,128)(2,1)S(1)}, bf16[2,128,64]{1,0,2:T(2,128)(2,1)S(1)}, u32[]{:S(2)}, u32[]{:S(2)}) %collective-permute-start.7) | collective-permute-done | bytes 32800 | tf_op jit(solution)/shard_map/ppermute | solution.py:86
  43.6 4.2 %collective-permute-done.8 = bf16[2,128,64]{1,0,2:T(2,128)(2,1)S(1)} collective-permute-done((bf16[2,128,64]{1,0,2:T(2,128)(2,1)S(1)}, bf16[2,128,64]{1,0,2:T(2,128)(2,1)S(1)}, u32[]{:S(2)}, u32[]{:S(2)}) %collective-permute-start.8) | collective-permute-done | bytes 32800 | tf_op jit(solution)/shard_map/ppermute | solution.py:86
  47.8 4.4 %collective-permute-done.9 = bf16[2,128,64]{1,0,2:T(2,128)(2,1)S(1)} collective-permute-done((bf16[2,128,64]{1,0,2:T(2,128)(2,1)S(1)}, bf16[2,128,64]{1,0,2:T(2,128)(2,1)S(1)}, u32[]{:S(2)}, u32[]{:S(2)}) %collective-permute-start.9) | collective-permute-done | bytes 32800 | tf_op jit(solution)/shard_map/ppermute | solution.py:86
  52.2 6.0 %collective-permute-done.10 = bf16[2,128,64]{1,0,2:T(2,128)(2,1)S(1)} collective-permute-done((bf16[2,128,64]{1,0,2:T(2,128)(2,1)S(1)}, bf16[2,128,64]{1,0,2:T(2,128)(2,1)S(1)}, u32[]{:S(2)}, u32[]{:S(2)}) %collective-permute-start.10) | collective-permute-done | bytes 32800 | tf_op jit(solution)/shard_map/ppermute | solution.py:86
  58.3 6.0 %collective-permute-done.11 = bf16[2,128,64]{1,0,2:T(2,128)(2,1)S(1)} collective-permute-done((bf16[2,128,64]{1,0,2:T(2,128)(2,1)S(1)}, bf16[2,128,64]{1,0,2:T(2,128)(2,1)S(1)}, u32[]{:S(2)}, u32[]{:S(2)}) %collective-permute-start.11) | collective-permute-done | bytes 32800 | tf_op jit(solution)/shard_map/ppermute | solution.py:86
  64.3 6.0 %collective-permute-done.12 = bf16[2,128,64]{1,0,2:T(2,128)(2,1)S(1)} collective-permute-done((bf16[2,128,64]{1,0,2:T(2,128)(2,1)S(1)}, bf16[2,128,64]{1,0,2:T(2,128)(2,1)S(1)}, u32[]{:S(2)}, u32[]{:S(2)}) %collective-permute-start.12) | collective-permute-done | bytes 32800 | tf_op jit(solution)/shard_map/ppermute | solution.py:86
  71.0 5.4 %collective-permute-done.13 = bf16[2,128,64]{1,0,2:T(2,128)(2,1)S(1)} collective-permute-done((bf16[2,128,64]{1,0,2:T(2,128)(2,1)S(1)}, bf16[2,128,64]{1,0,2:T(2,128)(2,1)S(1)}, u32[]{:S(2)}, u32[]{:S(2)}) %collective-permute-start.13) | collective-permute-done | bytes 32800 | tf_op jit(solution)/shard_map/ppermute | solution.py:86
  79.0 3.4 %collective-permute-done.14 = bf16[2,128,64]{1,0,2:T(2,128)(2,1)S(1)} collective-permute-done((bf16[2,128,64]{1,0,2:T(2,128)(2,1)S(1)}, bf16[2,128,64]{1,0,2:T(2,128)(2,1)S(1)}, u32[]{:S(2)}, u32[]{:S(2)}) %collective-permute-start.14) | collective-permute-done | bytes 32800 | tf_op jit(solution)/shard_map/ppermute | solution.py:86
  85.3 23.2 %while.20 = (s32[]{:T(128)}, f32[2,128,64]{1,2,0:T(8,128)S(1)}, s32[]{:T(128)}, s32[]{:T(128)}, s32[]{:T(128)}, /*index=5*/s32[96]{0:T(128)S(1)}, bf16[96,128,12...) while((s32[]{:T(128)}, f32[2,128,64]{1,2,0:T(8,128)S(1)}, ...), condition=%wide.region_4.5_spmd, body=%wide.region_2.4_spmd.sunk | while | flops 33687796 | bytes 4465817 | solution.py:21
  108.5 4.6 %all_gather.3 = bf16[256,128]{0,1:T(8,128)(2,1)S(1)} all-gather(bf16[256,64]{0,1:T(8,128)(2,1)S(1)} %copy_bitcast_fusion.1), channel_id=1, replica_groups=mesh['rows'=16,'cols'=2] {'cols'}, dimensions={1}, use_global_device_ids=true | all-gather | bytes 98304 | tf_op jit(solution)/shard_map/all_gather | solution.py:101
  114.0 48.9 %psum.15 = f32[128]{0:T(128)S(1)} all-reduce(f32[128]{0:T(128)S(1)} %get-tuple-element.167), channel_id=1, replica_groups=mesh['rows'=16,'cols'=2] {'rows'}, use_global_device_ids=true, to_apply=%region_7.8 | all-reduce | flops 128 | bytes 1024 | tf_op jit(solution)/shard_map/psum | solution.py:115
  165.2 9.3 %reduce-scatter.2.cloned.1.call-done = f32[256,64]{0,1:T(8,128)} async-done(((f32[256,128]{0,1:T(8,128)}), f32[256,64]{0,1:T(8,128)}) %reduce-scatter.2.cloned.1.call-update) | async-done | bytes 65552 | tf_op jit(solution)/shard_map/reduce_scatter | solution.py:123
  175.5 20.8 %while.21 = (s32[]{:T(128)}, f32[10,128,64]{1,2,0:T(8,128)S(1)}, s32[]{:T(128)}, s32[]{:T(128)}, s32[96]{0:T(128)S(1)}, /*index=5*/bf16[96,128,128]{2,1,0:T(8,12...) while((s32[]{:T(128)}, f32[10,128,64]{1,2,0:T(8,128)S(1)}, s32[]{:T(128)}, ...), condition=%wide.region_11.12_spmd, body=%wide.region_9.11_spmd.sunk | while | flops 33687776 | bytes 4465797 | solution.py:21
  176.9 2.6 gather_fusion.5
  183.8 2.6 gather_fusion.5
  199.1 21.3 %collective-permute-start.17 = (f32[2,128,64]{1,0,2:T(2,128)S(1)}, f32[2,128,64]{1,0,2:T(2,128)S(1)}, u32[]{:S(2)}, u32[]{:S(2)}) collective-permute-start(f32[2,128,64]{1,0,2:T(2,128)S(1)} %get-tuple-element.171), channel_id=1, source_target_pairs={{0,8},{2,10},{4,12},{6,14},{8,0},{10,2},{12,4},{14,6},{16,24},{18,... | collective-permute-start | bytes 196616 | tf_op jit(solution)/shard_map/ppermute | solution.py:11
  220.4 36.4 %all-reduce.2.cloned.1.call-done = f32[128,128]{1,0:T(8,128)} async-done(((f32[128,128]{1,0:T(8,128)}), f32[128,128]{1,0:T(8,128)}) %all-reduce.2.cloned.1.call-update) | async-done | bytes 65552 | tf_op jit(solution)/shard_map/psum | solution.py:115
  (121 shorter events, 51.5 us)
Async XLA Ops:
  8.0 105.1 %copy-start = (bf16[128,128]{1,0:T(8,128)(2,1)S(1)}, bf16[128,128]{1,0:T(8,128)(2,1)}, u32[]{:S(2)}) copy-start(bf16[128,128]{1,0:T(8,128)(2,1)} %param.19) | copy-start | bytes 98308
  8.0 77.2 %copy-start.2 = (s32[96]{0:T(128)S(1)}, s32[96]{0:T(128)}, u32[]{:S(2)}) copy-start(s32[96]{0:T(128)} %param.15) | copy-start | bytes 1156
  8.0 77.2 %copy-start.1 = (s32[96]{0:T(128)S(1)}, s32[96]{0:T(128)}, u32[]{:S(2)}) copy-start(s32[96]{0:T(128)} %param.16) | copy-start | bytes 1156
  8.0 166.4 %reduce-scatter.2.cloned.1.call-start = ((), (), s32[]{:S(2)}) async-start(), calls=%async_computation.2 | async-start | bytes 196608 | tf_op jit(solution)/shard_map/reduce_scatter | solution.py:123
  9.6 4.3 %collective-permute-start = (bf16[2,128,64]{1,0,2:T(2,128)(2,1)S(1)}, bf16[2,128,64]{1,0,2:T(2,128)(2,1)S(1)}, u32[]{:S(2)}, u32[]{:S(2)}) collective-permute-start(bf16[2,128,64]{1,0,2:T(2,128)(2,1)S(1)} %multiply_convert_fusion.3), channel_id=1, source_target_pairs={{0,2},{2,4},{4,6},{6,8},{8,10},{10,12},{12,14},{14,16},{16,18},{18... | collective-permute-start | bytes 98312 | tf_op jit(solution)/shard_map/ppermute | solution.py:86
  13.9 4.2 %collective-permute-start.1 = (bf16[2,128,64]{1,0,2:T(2,128)(2,1)S(1)}, bf16[2,128,64]{1,0,2:T(2,128)(2,1)S(1)}, u32[]{:S(2)}, u32[]{:S(2)}) collective-permute-start(bf16[2,128,64]{1,0,2:T(2,128)(2,1)S(1)} %collective-permute-done), channel_id=1, source_target_pairs={{0,2},{2,4},{4,6},{6,8},{8,10},{10,12},{12,14},{14,16},{16,18},{18... | collective-permute-start | bytes 98312 | tf_op jit(solution)/shard_map/ppermute | solution.py:86
  18.2 4.2 %collective-permute-start.2 = (bf16[2,128,64]{1,0,2:T(2,128)(2,1)S(1)}, bf16[2,128,64]{1,0,2:T(2,128)(2,1)S(1)}, u32[]{:S(2)}, u32[]{:S(2)}) collective-permute-start(bf16[2,128,64]{1,0,2:T(2,128)(2,1)S(1)} %collective-permute-done.1), channel_id=1, source_target_pairs={{0,2},{2,4},{4,6},{6,8},{8,10},{10,12},{12,14},{14,16},{16,18},{18... | collective-permute-start | bytes 98312 | tf_op jit(solution)/shard_map/ppermute | solution.py:86
  22.4 4.2 %collective-permute-start.3 = (bf16[2,128,64]{1,0,2:T(2,128)(2,1)S(1)}, bf16[2,128,64]{1,0,2:T(2,128)(2,1)S(1)}, u32[]{:S(2)}, u32[]{:S(2)}) collective-permute-start(bf16[2,128,64]{1,0,2:T(2,128)(2,1)S(1)} %collective-permute-done.2), channel_id=1, source_target_pairs={{0,2},{2,4},{4,6},{6,8},{8,10},{10,12},{12,14},{14,16},{16,18},{18... | collective-permute-start | bytes 98312 | tf_op jit(solution)/shard_map/ppermute | solution.py:86
  26.6 4.2 %collective-permute-start.4 = (bf16[2,128,64]{1,0,2:T(2,128)(2,1)S(1)}, bf16[2,128,64]{1,0,2:T(2,128)(2,1)S(1)}, u32[]{:S(2)}, u32[]{:S(2)}) collective-permute-start(bf16[2,128,64]{1,0,2:T(2,128)(2,1)S(1)} %collective-permute-done.3), channel_id=1, source_target_pairs={{0,2},{2,4},{4,6},{6,8},{8,10},{10,12},{12,14},{14,16},{16,18},{18... | collective-permute-start | bytes 98312 | tf_op jit(solution)/shard_map/ppermute | solution.py:86
  30.9 4.2 %collective-permute-start.5 = (bf16[2,128,64]{1,0,2:T(2,128)(2,1)S(1)}, bf16[2,128,64]{1,0,2:T(2,128)(2,1)S(1)}, u32[]{:S(2)}, u32[]{:S(2)}) collective-permute-start(bf16[2,128,64]{1,0,2:T(2,128)(2,1)S(1)} %collective-permute-done.4), channel_id=1, source_target_pairs={{0,2},{2,4},{4,6},{6,8},{8,10},{10,12},{12,14},{14,16},{16,18},{18... | collective-permute-start | bytes 98312 | tf_op jit(solution)/shard_map/ppermute | solution.py:86
  35.1 4.2 %collective-permute-start.6 = (bf16[2,128,64]{1,0,2:T(2,128)(2,1)S(1)}, bf16[2,128,64]{1,0,2:T(2,128)(2,1)S(1)}, u32[]{:S(2)}, u32[]{:S(2)}) collective-permute-start(bf16[2,128,64]{1,0,2:T(2,128)(2,1)S(1)} %collective-permute-done.5), channel_id=1, source_target_pairs={{0,2},{2,4},{4,6},{6,8},{8,10},{10,12},{12,14},{14,16},{16,18},{18... | collective-permute-start | bytes 98312 | tf_op jit(solution)/shard_map/ppermute | solution.py:86
  39.4 4.2 %collective-permute-start.7 = (bf16[2,128,64]{1,0,2:T(2,128)(2,1)S(1)}, bf16[2,128,64]{1,0,2:T(2,128)(2,1)S(1)}, u32[]{:S(2)}, u32[]{:S(2)}) collective-permute-start(bf16[2,128,64]{1,0,2:T(2,128)(2,1)S(1)} %collective-permute-done.6), channel_id=1, source_target_pairs={{0,2},{2,4},{4,6},{6,8},{8,10},{10,12},{12,14},{14,16},{16,18},{18... | collective-permute-start | bytes 98312 | tf_op jit(solution)/shard_map/ppermute | solution.py:86
  43.6 4.2 %collective-permute-start.8 = (bf16[2,128,64]{1,0,2:T(2,128)(2,1)S(1)}, bf16[2,128,64]{1,0,2:T(2,128)(2,1)S(1)}, u32[]{:S(2)}, u32[]{:S(2)}) collective-permute-start(bf16[2,128,64]{1,0,2:T(2,128)(2,1)S(1)} %collective-permute-done.7), channel_id=1, source_target_pairs={{0,2},{2,4},{4,6},{6,8},{8,10},{10,12},{12,14},{14,16},{16,18},{18... | collective-permute-start | bytes 98312 | tf_op jit(solution)/shard_map/ppermute | solution.py:86
  47.8 4.4 %collective-permute-start.9 = (bf16[2,128,64]{1,0,2:T(2,128)(2,1)S(1)}, bf16[2,128,64]{1,0,2:T(2,128)(2,1)S(1)}, u32[]{:S(2)}, u32[]{:S(2)}) collective-permute-start(bf16[2,128,64]{1,0,2:T(2,128)(2,1)S(1)} %collective-permute-done.8), channel_id=1, source_target_pairs={{0,2},{2,4},{4,6},{6,8},{8,10},{10,12},{12,14},{14,16},{16,18},{18... | collective-permute-start | bytes 98312 | tf_op jit(solution)/shard_map/ppermute | solution.py:86
  52.2 6.0 %collective-permute-start.10 = (bf16[2,128,64]{1,0,2:T(2,128)(2,1)S(1)}, bf16[2,128,64]{1,0,2:T(2,128)(2,1)S(1)}, u32[]{:S(2)}, u32[]{:S(2)}) collective-permute-start(bf16[2,128,64]{1,0,2:T(2,128)(2,1)S(1)} %collective-permute-done.9), channel_id=1, source_target_pairs={{0,2},{2,4},{4,6},{6,8},{8,10},{10,12},{12,14},{14,16},{16,18},{18... | collective-permute-start | bytes 98312 | tf_op jit(solution)/shard_map/ppermute | solution.py:86
  58.3 6.0 %collective-permute-start.11 = (bf16[2,128,64]{1,0,2:T(2,128)(2,1)S(1)}, bf16[2,128,64]{1,0,2:T(2,128)(2,1)S(1)}, u32[]{:S(2)}, u32[]{:S(2)}) collective-permute-start(bf16[2,128,64]{1,0,2:T(2,128)(2,1)S(1)} %collective-permute-done.10), channel_id=1, source_target_pairs={{0,2},{2,4},{4,6},{6,8},{8,10},{10,12},{12,14},{14,16},{16,18},{18... | collective-permute-start | bytes 98312 | tf_op jit(solution)/shard_map/ppermute | solution.py:86
  64.3 6.0 %collective-permute-start.12 = (bf16[2,128,64]{1,0,2:T(2,128)(2,1)S(1)}, bf16[2,128,64]{1,0,2:T(2,128)(2,1)S(1)}, u32[]{:S(2)}, u32[]{:S(2)}) collective-permute-start(bf16[2,128,64]{1,0,2:T(2,128)(2,1)S(1)} %collective-permute-done.11), channel_id=1, source_target_pairs={{0,2},{2,4},{4,6},{6,8},{8,10},{10,12},{12,14},{14,16},{16,18},{18... | collective-permute-start | bytes 98312 | tf_op jit(solution)/shard_map/ppermute | solution.py:86
  70.3 6.0 %collective-permute-start.13 = (bf16[2,128,64]{1,0,2:T(2,128)(2,1)S(1)}, bf16[2,128,64]{1,0,2:T(2,128)(2,1)S(1)}, u32[]{:S(2)}, u32[]{:S(2)}) collective-permute-start(bf16[2,128,64]{1,0,2:T(2,128)(2,1)S(1)} %collective-permute-done.12), channel_id=1, source_target_pairs={{0,2},{2,4},{4,6},{6,8},{8,10},{10,12},{12,14},{14,16},{16,18},{18... | collective-permute-start | bytes 98312 | tf_op jit(solution)/shard_map/ppermute | solution.py:86
  76.4 6.0 %collective-permute-start.14 = (bf16[2,128,64]{1,0,2:T(2,128)(2,1)S(1)}, bf16[2,128,64]{1,0,2:T(2,128)(2,1)S(1)}, u32[]{:S(2)}, u32[]{:S(2)}) collective-permute-start(bf16[2,128,64]{1,0,2:T(2,128)(2,1)S(1)} %collective-permute-done.13), channel_id=1, source_target_pairs={{0,2},{2,4},{4,6},{6,8},{8,10},{10,12},{12,14},{14,16},{16,18},{18... | collective-permute-start | bytes 98312 | tf_op jit(solution)/shard_map/ppermute | solution.py:86
  163.8 93.1 %all-reduce.2.cloned.1.call-start = ((), (), s32[]{:S(2)}) async-start(), calls=%async_computation.1 | async-start | bytes 131072 | tf_op jit(solution)/shard_map/psum | solution.py:115
  196.6 61.7 %collective-permute-start.18 = (f32[2,128,64]{1,0,2:T(2,128)S(1)}, f32[2,128,64]{1,0,2:T(2,128)S(1)}, u32[]{:S(2)}, u32[]{:S(2)}) collective-permute-start(f32[2,128,64]{1,0,2:T(2,128)S(1)} %get-tuple-element.170), channel_id=1, source_target_pairs={{0,16},{2,18},{4,20},{6,22},{8,24},{10,26},{12,28},{14,30},{16,0},... | collective-permute-start | bytes 196616 | tf_op jit(solution)/shard_map/ppermute | solution.py:11
  199.1 59.3 %collective-permute-start.17 = (f32[2,128,64]{1,0,2:T(2,128)S(1)}, f32[2,128,64]{1,0,2:T(2,128)S(1)}, u32[]{:S(2)}, u32[]{:S(2)}) collective-permute-start(f32[2,128,64]{1,0,2:T(2,128)S(1)} %get-tuple-element.171), channel_id=1, source_target_pairs={{0,8},{2,10},{4,12},{6,14},{8,0},{10,2},{12,4},{14,6},{16,24},{18,... | collective-permute-start | bytes 196616 | tf_op jit(solution)/shard_map/ppermute | solution.py:11
  220.4 37.9 %collective-permute-start.16 = (f32[2,128,64]{1,0,2:T(2,128)S(1)}, f32[2,128,64]{1,0,2:T(2,128)S(1)}, u32[]{:S(2)}, u32[]{:S(2)}) collective-permute-start(f32[2,128,64]{1,0,2:T(2,128)S(1)} %get-tuple-element.172), channel_id=1, source_target_pairs={{0,4},{2,6},{4,0},{6,2},{8,12},{10,14},{12,8},{14,10},{16,20},{18,... | collective-permute-start | bytes 196616 | tf_op jit(solution)/shard_map/ppermute | solution.py:11
  220.4 37.9 %collective-permute-start.15 = (f32[2,128,64]{1,0,2:T(2,128)S(1)}, f32[2,128,64]{1,0,2:T(2,128)S(1)}, u32[]{:S(2)}, u32[]{:S(2)}) collective-permute-start(f32[2,128,64]{1,0,2:T(2,128)S(1)} %get-tuple-element.169), channel_id=1, source_target_pairs={{0,2},{2,0},{4,6},{6,4},{8,10},{10,8},{12,14},{14,12},{16,18},{18,... | collective-permute-start | bytes 196616 | tf_op jit(solution)/shard_map/ppermute | solution.py:11
  (2 other events, 55.7 us)
Sparse Core Ops, SparseCore 0:
  163.9 10.5 reduce-scatter.1
Sparse Core Ops, SparseCore 1:
  168.3 88.5 all-reduce.1
